TPU v7x, 32 devices: a whole 2x2x4 slice. The times are simulated.
32 devices in a mesh: grp: 4 (over y, x), ep: 8 (over z, core).
Axes of the slice: x: 2, y: 2, z: 4, core: 2. Of those that a mesh axis runs over, the one named last changes fastest.
Arguments:
- layer_input: bfloat16 [8192, 8192], P(('grp', 'ep')), may hold values from -6 to 6
- output_grad: bfloat16 [8192, 8192], P(('grp', 'ep')), may hold values from -0.119628906 to 0.119628906
- adapter_ids: int32 [8192, 1], P(('grp', 'ep')), may hold values from 0 to 7; in each aligned block of 256 rows (0 to 255, 256 to 511, ...) at most 64 rows name the same one
- owner_map: int32 [8], replicated, may hold values from 0 to 7, each once
- weights: bfloat16 [8, 2, 64, 8192], P('ep', None, None, 'grp'), may hold values from -0.0625 to 0.0625
- moment: float32 [8, 2, 64, 8192], P('ep', None, None, 'grp'), may hold values from -1.8 to 1.8
- second: float32 [8, 2, 64, 8192], P('ep', None, None, 'grp'), may hold values from 0.0002 to 0.004
Outputs:
- moment_next: float32 [8, 2, 64, 8192], P('ep', None, None, 'grp')
- second_next: float32 [8, 2, 64, 8192], P('ep', None, None, 'grp')
- direction: float32 [8, 2, 64, 8192], P('ep', None, None, 'grp')
Inputs may be any that keep to these rules, and one draw needn't show every extreme that they name: `adapter_ids`: among the rows of one device no adapter appears more than 64 times, and some adapter appears exactly 64 times. `owner_map`: each owner index appears once.
All inputs are finite; a program needn't handle non-finite values.
Results may differ from a plain program's by a relative error of at most 0.0026.
Values may be sent and summed in bfloat16 or wider, within the bound.
No kernel may reach another device: no remote copies, remote signals or barrier semaphores. Data moves between devices by JAX's collectives and lax.ppermute only.
A program may use at most 128 MiB of HBM per device.

v0:
```python
import jax
import jax.numpy as jnp
from jax import lax
from jax.sharding import PartitionSpec as P

STEP = 100
ADAPTER_SCALING = 2.0
BETA_FIRST = 0.9
BETA_SECOND = 0.999
ADAM_EPSILON = 1e-08
FEATURE_CHUNKS = 4
RANK_CHUNKS = 2


def swap(values, axis, step):
    count = lax.axis_size(axis)
    return lax.ppermute(values, axis, [(i, i ^ step) for i in range(count)])


def tie(value, *others):
    return lax.optimization_barrier((value, *others))[0]


def adam_step(grads, moment, second):
    moment_next = BETA_FIRST * moment + (1.0 - BETA_FIRST) * grads
    second_next = BETA_SECOND * second + (1.0 - BETA_SECOND) * grads * grads
    first_fix = 1.0 - BETA_FIRST**STEP
    second_fix = 1.0 - BETA_SECOND**STEP
    direction = moment_next / first_fix / (jnp.sqrt(second_next / second_fix) + ADAM_EPSILON)
    return (moment_next, second_next, direction)


def gather_owners(own):
    count = lax.axis_size("ep")
    even = [own] + [swap(own, "ep", k) for k in range(2, count, 2)]
    even = jnp.stack(even)
    odd = swap(even, "ep", 1)
    return jnp.stack([even, odd], axis=1).reshape((count,) + own.shape)


def scatter_owners(partial):
    count = lax.axis_size("ep")
    pairs = partial.reshape((count // 2, 2) + partial.shape[1:])
    here = pairs[:, 0] + swap(pairs[:, 1].astype(jnp.bfloat16), "ep", 1).astype(jnp.float32)
    total = here[0]
    sent = here.astype(jnp.bfloat16)
    for k in range(1, count // 2):
        total = total + swap(sent[k], "ep", 2 * k).astype(jnp.float32)
    return total


def per_device(layer_input, output_grad, adapter_ids, owner_map, weights, moment, second):
    groups = lax.axis_size("grp")
    owners = lax.axis_size("ep")
    mine = lax.axis_index("grp")
    me = lax.axis_index("ep")
    rows, width = layer_input.shape
    part = width // groups
    rank = weights.shape[2]

    def piece(array, step, chunk, chunks):
        size = part // chunks
        return lax.dynamic_slice(array, (0, (mine ^ step) * part + chunk * size), (rows, size))

    def send(array, chunk, chunks, after=None):
        out = [piece(array, 0, chunk, chunks)]
        for d in range(1, groups):
            block = piece(array, d, chunk, chunks)
            if after is not None:
                block = tie(block, after)
            out.append(swap(block, "grp", d))
        return jnp.concatenate(out)

    og = send(output_grad, 0, 1)
    li = [send(layer_input, 0, FEATURE_CHUNKS)]

    hot = adapter_ids[:, 0][None, :] == jnp.arange(owner_map.shape[0], dtype=jnp.int32)[:, None]
    owner_of = jnp.sum(jnp.where(hot, owner_map[:, None], 0), axis=0)
    owner_of = jnp.concatenate([owner_of] + [swap(owner_of, "grp", d) for d in range(1, groups)])
    relative = owner_of ^ me
    mask = relative[None, :] == jnp.arange(owners, dtype=jnp.int32)[:, None]

    def low_part(matrix, values):
        every = lax.dot_general(
            matrix.reshape(owners * rank, -1), values, (((1,), (1,)), ((), ())), preferred_element_type=jnp.float32
        ).reshape(owners, rank, -1)
        return jnp.sum(jnp.where(mask[:, None, :], every, 0.0), axis=0)

    def blocks(low):
        return [low[:, b * rows : (b + 1) * rows] for b in range(groups)]

    def sum_two_stage(low):
        part_of = blocks(low)
        total = part_of[0]
        for d in range(1, groups):
            total = total + swap(part_of[d], "grp", d)
        total = total.astype(jnp.bfloat16)
        return jnp.concatenate([total] + [swap(total, "grp", d) for d in range(1, groups)], axis=1)

    def sum_direct(low):
        got = [blocks(low)] + [blocks(swap(low, "grp", d)) for d in range(1, groups)]
        out = []
        for b in range(groups):
            total = got[0][b]
            for d in range(1, groups):
                total = total + got[d][b ^ d]
            out.append(total)
        return jnp.concatenate(out, axis=1).astype(jnp.bfloat16)

    def outer(low, values):
        spread = jnp.where(mask[:, None, :], low[None], jnp.zeros((), low.dtype))
        return ADAPTER_SCALING * lax.dot_general(
            spread.reshape(-1, low.shape[1]), values, (((1,), (0,)), ((), ())), preferred_element_type=jnp.float32
        ).reshape(owners, low.shape[0], -1)

    cut = part // FEATURE_CHUNKS
    up = gather_owners(weights[0, 1])
    down = gather_owners(weights[0, 0])
    low_grad = sum_two_stage(low_part(up, og))
    for c in range(1, FEATURE_CHUNKS):
        li.append(send(layer_input, c, FEATURE_CHUNKS))
    low_in = None
    for c in range(FEATURE_CHUNKS):
        p = low_part(down[:, :, c * cut : (c + 1) * cut], li[c])
        low_in = p if low_in is None else low_in + p
    down_grads = []
    half = FEATURE_CHUNKS // 2
    pair = jnp.concatenate([outer(low_grad, li[c]) for c in range(half)], axis=2)
    down_grads.append(scatter_owners(pair))
    for c in range(half, FEATURE_CHUNKS):
        down_grads.append(scatter_owners(outer(low_grad, li[c])))
    down_grad = jnp.concatenate(down_grads, axis=1)
    size = rank // RANK_CHUNKS
    up_grads = []
    for r in range(RANK_CHUNKS):
        low = sum_direct(low_in[r * size : (r + 1) * size])
        up_grads.append(scatter_owners(outer(low, og)))
    up_grad = jnp.concatenate(up_grads, axis=0)
    grads = jnp.stack([down_grad, up_grad])[None]
    return adam_step(grads, moment, second)


def solution(mesh):
    rows = P(("grp", "ep"), None)
    held = P("ep", None, None, "grp")

    return jax.shard_map(
        per_device,
        mesh=mesh,
        in_specs=(rows, rows, rows, P(), held, held, held),
        out_specs=(held, held, held),
        check_vma=False,
    )
```

profile of v0, /device:TPU:0, one launch (start us, length us, event | category | flops | bytes accessed | tf_op | source)
XLA Modules:
  0.0 219.5 jit_solution(10574874486574411675)
XLA Ops:
  2.5 5.1 %collective-permute-start.5 = (bf16[64,2048]{1,0:T(8,128)(2,1)S(1)}, bf16[64,2048]{1,0:T(8,128)(2,1)S(1)}, u32[]{:S(2)}, u32[]{:S(2)}) collective-permute-start(bf16[64,2048]{1,0:T(8,128)(2,1)S(1)} %get-tuple-element.52), channel_id=1, source_target_pairs={{0,6},{1,7},{2,4},{3,5},{4,2},{5,3},{6,0},{7,1},{8,14},{9,15},{10,... | collective-permute-start | bytes 786440 | tf_op jit(solution)/shard_map/ppermute | solution.py:17
  8.9 2.7 %collective-permute-start.2 = (s32[256]{0:T(256)S(1)}, s32[256]{0:T(256)S(1)}, u32[]{:S(2)}, u32[]{:S(2)}) collective-permute-start(s32[256]{0:T(256)S(1)} %select_reduce_fusion.5), channel_id=1, source_target_pairs={{0,24},{8,16},{16,8},{24,0},{1,25},{9,17},{17,9},{25,1},{2,26},{10... | collective-permute-start | bytes 3080 | tf_op jit(solution)/shard_map/ppermute | solution.py:17
  12.1 2.8 %collective-permute-done.5 = bf16[64,2048]{1,0:T(8,128)(2,1)S(1)} collective-permute-done((bf16[64,2048]{1,0:T(8,128)(2,1)S(1)}, bf16[64,2048]{1,0:T(8,128)(2,1)S(1)}, u32[]{:S(2)}, u32[]{:S(2)}) %collective-permute-start.5) | collective-permute-done | bytes 262176 | tf_op jit(solution)/shard_map/ppermute | solution.py:17
  14.9 3.8 %collective-permute-start.42 = (bf16[64,2048]{1,0:T(8,128)(2,1)}, bf16[64,2048]{1,0:T(8,128)(2,1)}, u32[]{:S(2)}, u32[]{:S(2)}) collective-permute-start(bf16[64,2048]{1,0:T(8,128)(2,1)} %get-tuple-element.53), channel_id=1, source_target_pairs={{0,6},{1,7},{2,4},{3,5},{4,2},{5,3},{6,0},{7,1},{8,14},{9,15},{10,... | collective-permute-start | bytes 786440 | tf_op jit(solution)/shard_map/ppermute | solution.py:17
  18.7 17.8 %collective-permute-done.4 = bf16[64,2048]{1,0:T(8,128)(2,1)S(1)} collective-permute-done((bf16[64,2048]{1,0:T(8,128)(2,1)S(1)}, bf16[64,2048]{1,0:T(8,128)(2,1)S(1)}, u32[]{:S(2)}, u32[]{:S(2)}) %collective-permute-start.4) | collective-permute-done | bytes 262176 | tf_op jit(solution)/shard_map/ppermute | solution.py:17
  37.6 3.9 %constant_dynamic-slice_fusion.19 = (bf16[256,2048]{1,0:T(8,128)(2,1)S(1)}, bf16[256,2048]{1,0:T(8,128)(2,1)}, bf16[256,2048]{1,0:T(8,128)(2,1)}, bf16[256,2048]{1,0:T(8,128)(2,1)S(1)}) fusion(bf16[256,8192]{1,0:T(8,128)(2,1)} %param.8, s32[]{:T(128)S(6)} %select_n.96, s32[]{:T(128)S(6)} %select_n.97, s32[]{:T(128)S(6)} %select_n.99, s32[]{:T(128)S(6)} %select_n.98), kind=kLoop, calls=%fused_computation.181 | loop fusion | bytes 8388624 | tf_op jit(solution)/shard_map/dynamic_slice | solution.py:63
  48.1 2.6 %constant_dynamic-slice_fusion.11 = (bf16[256,512]{1,0:T(8,128)(2,1)S(1)}, bf16[256,512]{1,0:T(8,128)(2,1)S(1)}, bf16[256,512]{1,0:T(8,128)(2,1)S(1)}, bf16[256,...) fusion(bf16[256,8192]{1,0:T(8,128)(2,1)} %param.7, ...), kind=kLoop, calls=%fused_computation.173 | loop fusion | bytes 8388672 | tf_op jit(solution)/shard_map/dynamic_slice | solution.py:63
  54.0 6.1 %collective-permute-done.40 = bf16[64,2048]{1,0:T(8,128)(2,1)S(1)} collective-permute-done((bf16[64,2048]{1,0:T(8,128)(2,1)}, bf16[64,2048]{1,0:T(8,128)(2,1)S(1)}, u32[]{:S(2)}, u32[]{:S(2)}) %collective-permute-start.40) | collective-permute-done | bytes 262176 | tf_op jit(solution)/shard_map/ppermute | solution.py:17
  64.4 4.9 %collective-permute-done.7 = bf16[256,2048]{1,0:T(8,128)(2,1)S(1)} collective-permute-done((bf16[256,2048]{1,0:T(8,128)(2,1)}, bf16[256,2048]{1,0:T(8,128)(2,1)S(1)}, u32[]{:S(2)}, u32[]{:S(2)}) %collective-permute-start.7) | collective-permute-done | bytes 1048608 | tf_op jit(solution)/shard_map/ppermute | solution.py:17
  70.8 22.0 %collective-permute-done.9 = bf16[256,2048]{1,0:T(8,128)(2,1)S(1)} collective-permute-done((bf16[256,2048]{1,0:T(8,128)(2,1)}, bf16[256,2048]{1,0:T(8,128)(2,1)S(1)}, u32[]{:S(2)}, u32[]{:S(2)}) %collective-permute-start.9) | collective-permute-done | bytes 1048608 | tf_op jit(solution)/shard_map/ppermute | solution.py:17
  94.9 5.4 %select_reduce_fusion.4 = f32[64,1024]{1,0:T(8,128)S(1)} fusion(bf16[8,64,2048]{2,1,0:T(8,128)(2,1)S(1)} %bitcast.165, pred[8,1024]{1,0:T(8,128)(4,1)S(1)} %iota_compare_fusion, bf16[256,2048]{1,0:T(8,128)(2,1)S(1)} %collective-permute-done.9, bf16[256,2048]{1,0:T(8,128)(2,1)S(1)} %collective-permute-done.8, ...), kind=kOutput, calls=%fused_computation.18 | convolution fusion | flops 2165243904 | bytes 6561792 | tf_op jit(solution)/shard_map/dot_general | solution.py:84
  106.1 2.6 %collective-permute-done.26 = bf16[256,512]{1,0:T(8,128)(2,1)S(1)} collective-permute-done((bf16[256,512]{1,0:T(8,128)(2,1)S(1)}, bf16[256,512]{1,0:T(8,128)(2,1)S(1)}, u32[]{:S(2)}, u32[]{:S(2)}) %collective-permute-start.26) | collective-permute-done | bytes 262176 | tf_op jit(solution)/shard_map/ppermute | solution.py:17
  111.0 4.4 %collective-permute-done.21 = bf16[256,512]{1,0:T(8,128)(2,1)S(1)} collective-permute-done((bf16[256,512]{1,0:T(8,128)(2,1)S(1)}, bf16[256,512]{1,0:T(8,128)(2,1)S(1)}, u32[]{:S(2)}, u32[]{:S(2)}) %collective-permute-start.21) | collective-permute-done | bytes 262176 | tf_op jit(solution)/shard_map/ppermute | solution.py:17
  117.3 2.7 %collective-permute-done.19 = bf16[256,512]{1,0:T(8,128)(2,1)S(1)} collective-permute-done((bf16[256,512]{1,0:T(8,128)(2,1)S(1)}, bf16[256,512]{1,0:T(8,128)(2,1)S(1)}, u32[]{:S(2)}, u32[]{:S(2)}) %collective-permute-start.19) | collective-permute-done | bytes 262176 | tf_op jit(solution)/shard_map/ppermute | solution.py:17
  122.3 4.3 %collective-permute-done.18 = bf16[256,512]{1,0:T(8,128)(2,1)S(1)} collective-permute-done((bf16[256,512]{1,0:T(8,128)(2,1)S(1)}, bf16[256,512]{1,0:T(8,128)(2,1)S(1)}, u32[]{:S(2)}, u32[]{:S(2)}) %collective-permute-start.18) | collective-permute-done | bytes 262176 | tf_op jit(solution)/shard_map/ppermute | solution.py:17
  128.5 2.8 %collective-permute-done.16 = bf16[256,512]{1,0:T(8,128)(2,1)S(1)} collective-permute-done((bf16[256,512]{1,0:T(8,128)(2,1)S(1)}, bf16[256,512]{1,0:T(8,128)(2,1)S(1)}, u32[]{:S(2)}, u32[]{:S(2)}) %collective-permute-start.16) | collective-permute-done | bytes 262176 | tf_op jit(solution)/shard_map/ppermute | solution.py:17
  134.1 3.8 %collective-permute-done.35 = bf16[256,512]{1,0:T(8,128)(2,1)S(1)} collective-permute-done((bf16[256,512]{1,0:T(8,128)(2,1)S(1)}, bf16[256,512]{1,0:T(8,128)(2,1)S(1)}, u32[]{:S(2)}, u32[]{:S(2)}) %collective-permute-start.35) | collective-permute-done | bytes 262176 | tf_op jit(solution)/shard_map/ppermute | solution.py:17
  137.9 3.4 %collective-permute-done.34 = bf16[256,512]{1,0:T(8,128)(2,1)S(1)} collective-permute-done((bf16[256,512]{1,0:T(8,128)(2,1)S(1)}, bf16[256,512]{1,0:T(8,128)(2,1)S(1)}, u32[]{:S(2)}, u32[]{:S(2)}) %collective-permute-start.34) | collective-permute-done | bytes 262176 | tf_op jit(solution)/shard_map/ppermute | solution.py:17
  162.0 3.8 %collective-permute-start.37 = (bf16[64,512]{1,0:T(8,128)(2,1)S(1)}, bf16[64,512]{1,0:T(8,128)(2,1)S(1)}, u32[]{:S(2)}, u32[]{:S(2)}) collective-permute-start(bf16[64,512]{1,0:T(8,128)(2,1)S(1)} %get-tuple-element.64), channel_id=1, source_target_pairs={{0,2},{1,3},{2,0},{3,1},{4,6},{5,7},{6,4},{7,5},{8,10},{9,11},{10,... | collective-permute-start | bytes 196616 | tf_op jit(solution)/shard_map/ppermute | solution.py:17
  174.3 4.3 %collective-permute-done.32 = bf16[64,512]{1,0:T(8,128)(2,1)S(1)} collective-permute-done((bf16[64,512]{1,0:T(8,128)(2,1)S(1)}, bf16[64,512]{1,0:T(8,128)(2,1)S(1)}, u32[]{:S(2)}, u32[]{:S(2)}) %collective-permute-start.32) | collective-permute-done | bytes 65568 | tf_op jit(solution)/shard_map/ppermute | solution.py:17
  189.5 4.8 %collective-permute-start.48 = (bf16[32,2048]{1,0:T(8,128)(2,1)S(1)}, bf16[32,2048]{1,0:T(8,128)(2,1)S(1)}, u32[]{:S(2)}, u32[]{:S(2)}) collective-permute-start(bf16[32,2048]{1,0:T(8,128)(2,1)S(1)} %get-tuple-element.55), channel_id=1, source_target_pairs={{0,2},{1,3},{2,0},{3,1},{4,6},{5,7},{6,4},{7,5},{8,10},{9,11},{10,... | collective-permute-start | bytes 393224 | tf_op jit(solution)/shard_map/ppermute | solution.py:17
  194.3 7.6 %collective-permute-done.24 = bf16[64,1024]{1,0:T(8,128)(2,1)S(1)} collective-permute-done((bf16[64,1024]{1,0:T(8,128)(2,1)S(1)}, bf16[64,1024]{1,0:T(8,128)(2,1)S(1)}, u32[]{:S(2)}, u32[]{:S(2)}) %collective-permute-start.24) | collective-permute-done | bytes 131104 | tf_op jit(solution)/shard_map/ppermute | solution.py:17
  203.9 9.2 %collective-permute-done.56 = bf16[32,2048]{1,0:T(8,128)(2,1)S(1)} collective-permute-done((bf16[32,2048]{1,0:T(8,128)(2,1)S(1)}, bf16[32,2048]{1,0:T(8,128)(2,1)S(1)}, u32[]{:S(2)}, u32[]{:S(2)}) %collective-permute-start.56) | collective-permute-done | bytes 131104 | tf_op jit(solution)/shard_map/ppermute | solution.py:17
  213.2 4.1 %collective-permute-done.49 = bf16[32,2048]{1,0:T(8,128)(2,1)S(1)} collective-permute-done((bf16[32,2048]{1,0:T(8,128)(2,1)S(1)}, bf16[32,2048]{1,0:T(8,128)(2,1)S(1)}, u32[]{:S(2)}, u32[]{:S(2)}) %collective-permute-start.49) | collective-permute-done | bytes 131104 | tf_op jit(solution)/shard_map/ppermute | solution.py:17
  (152 shorter events, 83.6 us)
Async XLA Ops:
  7.6 28.9 %collective-permute-start.4 = (bf16[64,2048]{1,0:T(8,128)(2,1)S(1)}, bf16[64,2048]{1,0:T(8,128)(2,1)S(1)}, u32[]{:S(2)}, u32[]{:S(2)}) collective-permute-start(bf16[64,2048]{1,0:T(8,128)(2,1)S(1)} %get-tuple-element.52), channel_id=1, source_target_pairs={{0,4},{1,5},{2,6},{3,7},{4,0},{5,1},{6,2},{7,3},{8,12},{9,13},{10,... | collective-permute-start | bytes 786440 | tf_op jit(solution)/shard_map/ppermute | solution.py:17
  7.6 28.9 %collective-permute-start.3 = (bf16[64,2048]{1,0:T(8,128)(2,1)S(1)}, bf16[64,2048]{1,0:T(8,128)(2,1)S(1)}, u32[]{:S(2)}, u32[]{:S(2)}) collective-permute-start(bf16[64,2048]{1,0:T(8,128)(2,1)S(1)} %get-tuple-element.52), channel_id=1, source_target_pairs={{0,2},{1,3},{2,0},{3,1},{4,6},{5,7},{6,4},{7,5},{8,10},{9,11},{10,... | collective-permute-start | bytes 786440 | tf_op jit(solution)/shard_map/ppermute | solution.py:17
  8.9 32.6 %collective-permute-start.2 = (s32[256]{0:T(256)S(1)}, s32[256]{0:T(256)S(1)}, u32[]{:S(2)}, u32[]{:S(2)}) collective-permute-start(s32[256]{0:T(256)S(1)} %select_reduce_fusion.5), channel_id=1, source_target_pairs={{0,24},{8,16},{16,8},{24,0},{1,25},{9,17},{17,9},{25,1},{2,26},{10... | collective-permute-start | bytes 3080 | tf_op jit(solution)/shard_map/ppermute | solution.py:17
  11.6 31.5 %collective-permute-start.1 = (s32[256]{0:T(256)S(1)}, s32[256]{0:T(256)S(1)}, u32[]{:S(2)}, u32[]{:S(2)}) collective-permute-start(s32[256]{0:T(256)S(1)} %select_reduce_fusion.5), channel_id=1, source_target_pairs={{0,16},{8,24},{16,0},{24,8},{1,17},{9,25},{17,1},{25,9},{2,18},{10... | collective-permute-start | bytes 3080 | tf_op jit(solution)/shard_map/ppermute | solution.py:17
  14.9 32.7 %collective-permute-start.42 = (bf16[64,2048]{1,0:T(8,128)(2,1)}, bf16[64,2048]{1,0:T(8,128)(2,1)}, u32[]{:S(2)}, u32[]{:S(2)}) collective-permute-start(bf16[64,2048]{1,0:T(8,128)(2,1)} %get-tuple-element.53), channel_id=1, source_target_pairs={{0,6},{1,7},{2,4},{3,5},{4,2},{5,3},{6,0},{7,1},{8,14},{9,15},{10,... | collective-permute-start | bytes 786440 | tf_op jit(solution)/shard_map/ppermute | solution.py:17
  36.5 16.0 %collective-permute-start.41 = (bf16[64,2048]{1,0:T(8,128)(2,1)}, bf16[64,2048]{1,0:T(8,128)(2,1)}, u32[]{:S(2)}, u32[]{:S(2)}) collective-permute-start(bf16[64,2048]{1,0:T(8,128)(2,1)} %get-tuple-element.53), channel_id=1, source_target_pairs={{0,4},{1,5},{2,6},{3,7},{4,0},{5,1},{6,2},{7,3},{8,12},{9,13},{10,... | collective-permute-start | bytes 786440 | tf_op jit(solution)/shard_map/ppermute | solution.py:17
  37.6 25.1 %collective-permute-start.6 = (bf16[4,64,2048]{2,1,0:T(8,128)(2,1)}, bf16[4,64,2048]{2,1,0:T(8,128)(2,1)}, u32[]{:S(2)}, u32[]{:S(2)}) collective-permute-start(bf16[4,64,2048]{2,1,0:T(8,128)(2,1)} %get-tuple-element.37), channel_id=1, source_target_pairs={{0,1},{1,0},{2,3},{3,2},{4,5},{5,4},{6,7},{7,6},{8,9},{9,8},{10,11... | collective-permute-start | bytes 3145736 | tf_op jit(solution)/shard_map/ppermute | solution.py:17
  43.1 26.2 %collective-permute-start.7 = (bf16[256,2048]{1,0:T(8,128)(2,1)}, bf16[256,2048]{1,0:T(8,128)(2,1)S(1)}, u32[]{:S(2)}, u32[]{:S(2)}) collective-permute-start(bf16[256,2048]{1,0:T(8,128)(2,1)} %get-tuple-element.17), channel_id=1, source_target_pairs={{0,8},{8,0},{16,24},{24,16},{1,9},{9,1},{17,25},{25,17},{2,10},{10... | collective-permute-start | bytes 3145736 | tf_op jit(solution)/shard_map/ppermute | solution.py:17
  45.1 47.6 %collective-permute-start.9 = (bf16[256,2048]{1,0:T(8,128)(2,1)}, bf16[256,2048]{1,0:T(8,128)(2,1)S(1)}, u32[]{:S(2)}, u32[]{:S(2)}) collective-permute-start(bf16[256,2048]{1,0:T(8,128)(2,1)} %get-tuple-element.18), channel_id=1, source_target_pairs={{0,24},{8,16},{16,8},{24,0},{1,25},{9,17},{17,9},{25,1},{2,26},{10... | collective-permute-start | bytes 3145736 | tf_op jit(solution)/shard_map/ppermute | solution.py:17
  47.6 46.8 %collective-permute-start.8 = (bf16[256,2048]{1,0:T(8,128)(2,1)S(1)}, bf16[256,2048]{1,0:T(8,128)(2,1)S(1)}, u32[]{:S(2)}, u32[]{:S(2)}) collective-permute-start(bf16[256,2048]{1,0:T(8,128)(2,1)S(1)} %get-tuple-element.19), channel_id=1, source_target_pairs={{0,16},{8,24},{16,0},{24,8},{1,17},{9,25},{17,1},{25,9},{2,18},{10... | collective-permute-start | bytes 3145736 | tf_op jit(solution)/shard_map/ppermute | solution.py:17
  60.1 73.5 %collective-permute-start.33 = (bf16[256,512]{1,0:T(8,128)(2,1)S(1)}, bf16[256,512]{1,0:T(8,128)(2,1)S(1)}, u32[]{:S(2)}, u32[]{:S(2)}) collective-permute-start(bf16[256,512]{1,0:T(8,128)(2,1)S(1)} %get-tuple-element.21), channel_id=1, source_target_pairs={{0,8},{8,0},{16,24},{24,16},{1,9},{9,1},{17,25},{25,17},{2,10},{10... | collective-permute-start | bytes 786440 | tf_op jit(solution)/shard_map/ppermute | solution.py:17
  62.8 37.6 %collective-permute-start.43 = (bf16[4,64,2048]{2,1,0:T(8,128)(2,1)S(1)}, bf16[4,64,2048]{2,1,0:T(8,128)(2,1)S(1)}, u32[]{:S(2)}, u32[]{:S(2)}) collective-permute-start(bf16[4,64,2048]{2,1,0:T(8,128)(2,1)S(1)} %get-tuple-element.39), channel_id=1, source_target_pairs={{0,1},{1,0},{2,3},{3,2},{4,5},{5,4},{6,7},{7,6},{8,9},{9,8},{10,11... | collective-permute-start | bytes 3145736 | tf_op jit(solution)/shard_map/ppermute | solution.py:17
  69.3 34.8 %collective-permute-start.28 = (bf16[256,512]{1,0:T(8,128)(2,1)S(1)}, bf16[256,512]{1,0:T(8,128)(2,1)S(1)}, u32[]{:S(2)}, u32[]{:S(2)}) collective-permute-start(bf16[256,512]{1,0:T(8,128)(2,1)S(1)} %get-tuple-element.23), channel_id=1, source_target_pairs={{0,24},{8,16},{16,8},{24,0},{1,25},{9,17},{17,9},{25,1},{2,26},{10... | collective-permute-start | bytes 786440 | tf_op jit(solution)/shard_map/ppermute | solution.py:17
  100.4 14.9 %collective-permute-start.21 = (bf16[256,512]{1,0:T(8,128)(2,1)S(1)}, bf16[256,512]{1,0:T(8,128)(2,1)S(1)}, u32[]{:S(2)}, u32[]{:S(2)}) collective-permute-start(bf16[256,512]{1,0:T(8,128)(2,1)S(1)} %get-tuple-element.27), channel_id=1, source_target_pairs={{0,24},{8,16},{16,8},{24,0},{1,25},{9,17},{17,9},{25,1},{2,26},{10... | collective-permute-start | bytes 786440 | tf_op jit(solution)/shard_map/ppermute | solution.py:17
  108.7 17.9 %collective-permute-start.18 = (bf16[256,512]{1,0:T(8,128)(2,1)S(1)}, bf16[256,512]{1,0:T(8,128)(2,1)S(1)}, u32[]{:S(2)}, u32[]{:S(2)}) collective-permute-start(bf16[256,512]{1,0:T(8,128)(2,1)S(1)} %get-tuple-element.30), channel_id=1, source_target_pairs={{0,24},{8,16},{16,8},{24,0},{1,25},{9,17},{17,9},{25,1},{2,26},{10... | collective-permute-start | bytes 786440 | tf_op jit(solution)/shard_map/ppermute | solution.py:17
  120.0 17.9 %collective-permute-start.35 = (bf16[256,512]{1,0:T(8,128)(2,1)S(1)}, bf16[256,512]{1,0:T(8,128)(2,1)S(1)}, u32[]{:S(2)}, u32[]{:S(2)}) collective-permute-start(bf16[256,512]{1,0:T(8,128)(2,1)S(1)} %get-tuple-element.34), channel_id=1, source_target_pairs={{0,24},{8,16},{16,8},{24,0},{1,25},{9,17},{17,9},{25,1},{2,26},{10... | collective-permute-start | bytes 786440 | tf_op jit(solution)/shard_map/ppermute | solution.py:17
  126.6 14.6 %collective-permute-start.34 = (bf16[256,512]{1,0:T(8,128)(2,1)S(1)}, bf16[256,512]{1,0:T(8,128)(2,1)S(1)}, u32[]{:S(2)}, u32[]{:S(2)}) collective-permute-start(bf16[256,512]{1,0:T(8,128)(2,1)S(1)} %get-tuple-element.35), channel_id=1, source_target_pairs={{0,16},{8,24},{16,0},{24,8},{1,17},{9,25},{17,1},{25,9},{2,18},{10... | collective-permute-start | bytes 786440 | tf_op jit(solution)/shard_map/ppermute | solution.py:17
  159.6 20.5 %collective-permute-start.22 = (bf16[4,64,1024]{2,1,0:T(8,128)(2,1)S(1)}, bf16[4,64,1024]{2,1,0:T(8,128)(2,1)S(1)}, u32[]{:S(2)}, u32[]{:S(2)}) collective-permute-start(bf16[4,64,1024]{2,1,0:T(8,128)(2,1)S(1)} %fusion.28), channel_id=1, source_target_pairs={{0,1},{1,0},{2,3},{3,2},{4,5},{5,4},{6,7},{7,6},{8,9},{9,8},{10,11... | collective-permute-start | bytes 1572872 | tf_op jit(solution)/shard_map/ppermute | solution.py:17
  159.7 24.2 %collective-permute-start.54 = (bf16[4,32,2048]{2,1,0:T(8,128)(2,1)S(1)}, bf16[4,32,2048]{2,1,0:T(8,128)(2,1)S(1)}, u32[]{:S(2)}, u32[]{:S(2)}) collective-permute-start(bf16[4,32,2048]{2,1,0:T(8,128)(2,1)S(1)} %fusion.30), channel_id=1, source_target_pairs={{0,1},{1,0},{2,3},{3,2},{4,5},{5,4},{6,7},{7,6},{8,9},{9,8},{10,11... | collective-permute-start | bytes 1572872 | tf_op jit(solution)/shard_map/ppermute | solution.py:17
  182.3 19.6 %collective-permute-start.24 = (bf16[64,1024]{1,0:T(8,128)(2,1)S(1)}, bf16[64,1024]{1,0:T(8,128)(2,1)S(1)}, u32[]{:S(2)}, u32[]{:S(2)}) collective-permute-start(bf16[64,1024]{1,0:T(8,128)(2,1)S(1)} %get-tuple-element.50), channel_id=1, source_target_pairs={{0,4},{1,5},{2,6},{3,7},{4,0},{5,1},{6,2},{7,3},{8,12},{9,13},{10,... | collective-permute-start | bytes 393224 | tf_op jit(solution)/shard_map/ppermute | solution.py:17
  184.0 19.8 %collective-permute-start.55 = (bf16[32,2048]{1,0:T(8,128)(2,1)S(1)}, bf16[32,2048]{1,0:T(8,128)(2,1)S(1)}, u32[]{:S(2)}, u32[]{:S(2)}) collective-permute-start(bf16[32,2048]{1,0:T(8,128)(2,1)S(1)} %get-tuple-element.58), channel_id=1, source_target_pairs={{0,2},{1,3},{2,0},{3,1},{4,6},{5,7},{6,4},{7,5},{8,10},{9,11},{10,... | collective-permute-start | bytes 393224 | tf_op jit(solution)/shard_map/ppermute | solution.py:17
  185.1 18.9 %collective-permute-start.57 = (bf16[32,2048]{1,0:T(8,128)(2,1)S(1)}, bf16[32,2048]{1,0:T(8,128)(2,1)S(1)}, u32[]{:S(2)}, u32[]{:S(2)}) collective-permute-start(bf16[32,2048]{1,0:T(8,128)(2,1)S(1)} %get-tuple-element.59), channel_id=1, source_target_pairs={{0,6},{1,7},{2,4},{3,5},{4,2},{5,3},{6,0},{7,1},{8,14},{9,15},{10,... | collective-permute-start | bytes 393224 | tf_op jit(solution)/shard_map/ppermute | solution.py:17
  188.5 24.7 %collective-permute-start.56 = (bf16[32,2048]{1,0:T(8,128)(2,1)S(1)}, bf16[32,2048]{1,0:T(8,128)(2,1)S(1)}, u32[]{:S(2)}, u32[]{:S(2)}) collective-permute-start(bf16[32,2048]{1,0:T(8,128)(2,1)S(1)} %get-tuple-element.60), channel_id=1, source_target_pairs={{0,4},{1,5},{2,6},{3,7},{4,0},{5,1},{6,2},{7,3},{8,12},{9,13},{10,... | collective-permute-start | bytes 393224 | tf_op jit(solution)/shard_map/ppermute | solution.py:17
  189.5 23.7 %collective-permute-start.48 = (bf16[32,2048]{1,0:T(8,128)(2,1)S(1)}, bf16[32,2048]{1,0:T(8,128)(2,1)S(1)}, u32[]{:S(2)}, u32[]{:S(2)}) collective-permute-start(bf16[32,2048]{1,0:T(8,128)(2,1)S(1)} %get-tuple-element.55), channel_id=1, source_target_pairs={{0,2},{1,3},{2,0},{3,1},{4,6},{5,7},{6,4},{7,5},{8,10},{9,11},{10,... | collective-permute-start | bytes 393224 | tf_op jit(solution)/shard_map/ppermute | solution.py:17
  (36 other events, 344.4 us)
where the time goes:
time: 220 us
  waiting for transfers between devices  122 us (55%)
  starting transfers between devices  65.3 us (30%)
  matrix products  13.8 us (6%)
  local copies, waits for them, and re-layouts  9.21 us (4%)
  other arithmetic  8.14 us (4%)
    ppermute x58, waiting for transfers between devices, swap(): return lax.ppermute(values, axis, [(i, i ^ step) for i in range(count)])  122 us
    ppermute x58, starting transfers between devices, swap(): return lax.ppermute(values, axis, [(i, i ^ step) for i in range(count)])  65.3 us
    dot_general x5, matrix products, low_part(): lax.dot_general(matrix.reshape(owners * rank, -1), values, (((1,), (1,)),...  8.42 us
    dynamic_slice x2, local copies, waits for them, and re-layouts, piece(): lax.dynamic_slice(array, (0, (mine ^ step) * part + chunk * size), (rows,...  6.53 us
    dot_general x6, matrix products, outer(): lax.dot_general(spread.reshape(-1, low.shape[1]), values, (((1,), (0,)),...  5.34 us
  transfers between devices with their start and end apart: 58, of which 33 were waited for; matrix products, arithmetic and copies ran while one was open for 12% of the time, Pallas kernels for 0%

commit v1 on v0

--- a/solution.py
+++ b/solution.py
@@ -15,10 +15,6 @@
 def swap(values, axis, step):
     count = lax.axis_size(axis)
     return lax.ppermute(values, axis, [(i, i ^ step) for i in range(count)])
-
-
-def tie(value, *others):
-    return lax.optimization_barrier((value, *others))[0]
 
 
 def adam_step(grads, moment, second):
@@ -62,14 +58,14 @@
         size = part // chunks
         return lax.dynamic_slice(array, (0, (mine ^ step) * part + chunk * size), (rows, size))
 
-    def send(array, chunk, chunks, after=None):
-        out = [piece(array, 0, chunk, chunks)]
+    def send(array, chunk, chunks, single=False):
+        out = []
         for d in range(1, groups):
             block = piece(array, d, chunk, chunks)
-            if after is not None:
-                block = tie(block, after)
+            if single:
+                array, block = lax.optimization_barrier((array, block))
             out.append(swap(block, "grp", d))
-        return jnp.concatenate(out)
+        return jnp.concatenate([piece(array, 0, chunk, chunks)] + out)
 
     og = send(output_grad, 0, 1)
     li = [send(layer_input, 0, FEATURE_CHUNKS)]
@@ -131,10 +127,11 @@
         down_grads.append(scatter_owners(outer(low_grad, li[c])))
     down_grad = jnp.concatenate(down_grads, axis=1)
     size = rank // RANK_CHUNKS
+    og_all = lax.optimization_barrier(og)
     up_grads = []
     for r in range(RANK_CHUNKS):
         low = sum_direct(low_in[r * size : (r + 1) * size])
-        up_grads.append(scatter_owners(outer(low, og)))
+        up_grads.append(scatter_owners(outer(low, og_all)))
     up_grad = jnp.concatenate(up_grads, axis=0)
     grads = jnp.stack([down_grad, up_grad])[None]
     return adam_step(grads, moment, second)

time: 220 us -> 195 us (0.89)
  waiting for transfers between devices: 122 us -> 80.7 us
  starting transfers between devices: 65.3 us -> 78.1 us
  other arithmetic: 8.14 us -> 11.7 us
  matrix products: 13.8 us -> 10.7 us
  local copies, waits for them, and re-layouts: 9.21 us -> 11.9 us
    ppermute x58, waiting for transfers between devices: 122 us -> 80.7 us  [swap(): return lax.ppermute(values, axis, [(i, i ^ step) for i in range(count)])]
    ppermute x58, starting transfers between devices: 65.3 us -> 78.1 us  [swap(): return lax.ppermute(values, axis, [(i, i ^ step) for i in range(count)])]
    dot_general x5, matrix products: 8.42 us -> 5.36 us  [low_part(): lax.dot_general(matrix.reshape(owners * rank, -1), values, (((1,), (1,)),...]
    concatenate x0 -> x1, other arithmetic: none -> 2.31 us  [send(): return jnp.concatenate([piece(array, 0, chunk, chunks)] + out)]
  transfers between devices with their start and end apart: 58 -> 58, of which waited for: 33 -> 20; matrix products, arithmetic and copies ran while one was open for 12% -> 15% of each run, Pallas kernels for 0% -> 0%
where the time goes in v1:
time: 195 us
  waiting for transfers between devices  80.7 us (41%)
  starting transfers between devices  78.1 us (40%)
  local copies, waits for them, and re-layouts  11.9 us (6%)
  other arithmetic  11.7 us (6%)
  matrix products  10.7 us (5%)
    ppermute x58, waiting for transfers between devices, swap(): return lax.ppermute(values, axis, [(i, i ^ step) for i in range(count)])  80.7 us
    ppermute x58, starting transfers between devices, swap(): return lax.ppermute(values, axis, [(i, i ^ step) for i in range(count)])  78.1 us
    dynamic_slice x2, local copies, waits for them, and re-layouts, piece(): lax.dynamic_slice(array, (0, (mine ^ step) * part + chunk * size), (rows,...  8.24 us
    dot_general x5, matrix products, low_part(): lax.dot_general(matrix.reshape(owners * rank, -1), values, (((1,), (1,)),...  5.36 us
    dot_general x6, matrix products, outer(): lax.dot_general(spread.reshape(-1, low.shape[1]), values, (((1,), (0,)),...  5.34 us
    another operation x4, other arithmetic, gather_owners(): return jnp.stack([even, odd], axis=1).reshape((count,) + own.shape)  5.14 us
  transfers between devices with their start and end apart: 58, of which 20 were waited for; matrix products, arithmetic and copies ran while one was open for 15% of the time, Pallas kernels for 0%

profile of v1, /device:TPU:0, one launch (start us, length us, event | category | flops | bytes accessed | tf_op | source)
XLA Modules:
  0.0 194.6 jit_solution(6028280456310746934)
XLA Ops:
  2.6 3.1 %collective-permute-start.3 = (bf16[64,2048]{1,0:T(8,128)(2,1)S(1)}, bf16[64,2048]{1,0:T(8,128)(2,1)S(1)}, u32[]{:S(2)}, u32[]{:S(2)}) collective-permute-start(bf16[64,2048]{1,0:T(8,128)(2,1)S(1)} %get-tuple-element.52), channel_id=1, source_target_pairs={{0,2},{1,3},{2,0},{3,1},{4,6},{5,7},{6,4},{7,5},{8,10},{9,11},{10,... | collective-permute-start | bytes 786440 | tf_op jit(solution)/shard_map/ppermute | solution.py:17
  5.7 2.6 %collective-permute-start.4 = (bf16[64,2048]{1,0:T(8,128)(2,1)S(1)}, bf16[64,2048]{1,0:T(8,128)(2,1)}, u32[]{:S(2)}, u32[]{:S(2)}) collective-permute-start(bf16[64,2048]{1,0:T(8,128)(2,1)S(1)} %get-tuple-element.52), channel_id=1, source_target_pairs={{0,4},{1,5},{2,6},{3,7},{4,0},{5,1},{6,2},{7,3},{8,12},{9,13},{10,... | collective-permute-start | bytes 786440 | tf_op jit(solution)/shard_map/ppermute | solution.py:17
  11.4 3.9 %constant_dynamic-slice_fusion.19 = (bf16[256,2048]{1,0:T(8,128)(2,1)S(1)}, bf16[256,2048]{1,0:T(8,128)(2,1)}, bf16[256,2048]{1,0:T(8,128)(2,1)S(1)}, bf16[256,2048]{1,0:T(8,128)(2,1)}) fusion(bf16[256,8192]{1,0:T(8,128)(2,1)} %param.8, s32[]{:T(128)S(6)} %select_n.96, s32[]{:T(128)S(6)} %select_n.97, s32[]{:T(128)S(6)} %select_n.99, s32[]{:T(128)S(6)} %select_n.98), kind=kLoop, calls=%fused_computation.187 | loop fusion | bytes 8388624 | tf_op jit(solution)/shard_map/dynamic_slice | solution.py:59
  20.4 3.0 %collective-permute-done.2 = s32[256]{0:T(256)S(1)} collective-permute-done((s32[256]{0:T(256)S(1)}, s32[256]{0:T(256)S(1)}, u32[]{:S(2)}, u32[]{:S(2)}) %collective-permute-start.2) | collective-permute-done | bytes 1056 | tf_op jit(solution)/shard_map/ppermute | solution.py:17
  23.4 3.5 %collective-permute-start.41 = (bf16[64,2048]{1,0:T(8,128)(2,1)}, bf16[64,2048]{1,0:T(8,128)(2,1)}, u32[]{:S(2)}, u32[]{:S(2)}) collective-permute-start(bf16[64,2048]{1,0:T(8,128)(2,1)} %get-tuple-element.53), channel_id=1, source_target_pairs={{0,4},{1,5},{2,6},{3,7},{4,0},{5,1},{6,2},{7,3},{8,12},{9,13},{10,... | collective-permute-start | bytes 786440 | tf_op jit(solution)/shard_map/ppermute | solution.py:17
  32.7 4.3 %constant_dynamic-slice_fusion.11 = (bf16[256,512]{1,0:T(8,128)(2,1)}, bf16[256,512]{1,0:T(8,128)(2,1)}, bf16[256,512]{1,0:T(8,128)(2,1)}, bf16[256,512]{1,0:T(8...) fusion(bf16[256,8192]{1,0:T(8,128)(2,1)} %param.7, ...), kind=kLoop, calls=%fused_computation.179 | loop fusion | bytes 8388672 | tf_op jit(solution)/shard_map/dynamic_slice | solution.py:59
  37.1 5.5 %collective-permute-done.41 = bf16[64,2048]{1,0:T(8,128)(2,1)} collective-permute-done((bf16[64,2048]{1,0:T(8,128)(2,1)}, bf16[64,2048]{1,0:T(8,128)(2,1)}, u32[]{:S(2)}, u32[]{:S(2)}) %collective-permute-start.41) | collective-permute-done | bytes 262176 | tf_op jit(solution)/shard_map/ppermute | solution.py:17
  42.6 2.5 %collective-permute-start.42 = (bf16[64,2048]{1,0:T(8,128)(2,1)}, bf16[64,2048]{1,0:T(8,128)(2,1)S(1)}, u32[]{:S(2)}, u32[]{:S(2)}) collective-permute-start(bf16[64,2048]{1,0:T(8,128)(2,1)} %get-tuple-element.53), channel_id=1, source_target_pairs={{0,6},{1,7},{2,4},{3,5},{4,2},{5,3},{6,0},{7,1},{8,14},{9,15},{10,... | collective-permute-start | bytes 786440 | tf_op jit(solution)/shard_map/ppermute | solution.py:17
  45.1 6.6 %collective-permute-done.42 = bf16[64,2048]{1,0:T(8,128)(2,1)S(1)} collective-permute-done((bf16[64,2048]{1,0:T(8,128)(2,1)}, bf16[64,2048]{1,0:T(8,128)(2,1)S(1)}, u32[]{:S(2)}, u32[]{:S(2)}) %collective-permute-start.42) | collective-permute-done | bytes 262176 | tf_op jit(solution)/shard_map/ppermute | solution.py:17
  56.0 9.8 %collective-permute-done.8 = bf16[256,2048]{1,0:T(8,128)(2,1)} collective-permute-done((bf16[256,2048]{1,0:T(8,128)(2,1)}, bf16[256,2048]{1,0:T(8,128)(2,1)}, u32[]{:S(2)}, u32[]{:S(2)}) %collective-permute-start.8) | collective-permute-done | bytes 1048608 | tf_op jit(solution)/shard_map/ppermute | solution.py:17
  65.8 4.4 %collective-permute-start.19 = (bf16[256,512]{1,0:T(8,128)(2,1)S(1)}, bf16[256,512]{1,0:T(8,128)(2,1)S(1)}, u32[]{:S(2)}, u32[]{:S(2)}) collective-permute-start(bf16[256,512]{1,0:T(8,128)(2,1)S(1)} %copy-done.18), channel_id=1, source_target_pairs={{0,8},{8,0},{16,24},{24,16},{1,9},{9,1},{17,25},{25,17},{2,10},{10... | collective-permute-start | bytes 786440 | tf_op jit(solution)/shard_map/ppermute | solution.py:17
  70.2 6.6 %collective-permute-done.9 = bf16[256,2048]{1,0:T(8,128)(2,1)} collective-permute-done((bf16[256,2048]{1,0:T(8,128)(2,1)S(1)}, bf16[256,2048]{1,0:T(8,128)(2,1)}, u32[]{:S(2)}, u32[]{:S(2)}) %collective-permute-start.9) | collective-permute-done | bytes 1048608 | tf_op jit(solution)/shard_map/ppermute | solution.py:17
  87.8 11.7 %collective-permute-done.20 = bf16[256,512]{1,0:T(8,128)(2,1)S(1)} collective-permute-done((bf16[256,512]{1,0:T(8,128)(2,1)S(1)}, bf16[256,512]{1,0:T(8,128)(2,1)S(1)}, u32[]{:S(2)}, u32[]{:S(2)}) %collective-permute-start.20) | collective-permute-done | bytes 262176 | tf_op jit(solution)/shard_map/ppermute | solution.py:17
  101.0 2.9 %collective-permute-start.28 = (bf16[256,512]{1,0:T(8,128)(2,1)S(1)}, bf16[256,512]{1,0:T(8,128)(2,1)S(1)}, u32[]{:S(2)}, u32[]{:S(2)}) collective-permute-start(bf16[256,512]{1,0:T(8,128)(2,1)S(1)} %copy-done.11), channel_id=1, source_target_pairs={{0,24},{8,16},{16,8},{24,0},{1,25},{9,17},{17,9},{25,1},{2,26},{10... | collective-permute-start | bytes 786440 | tf_op jit(solution)/shard_map/ppermute | solution.py:17
  105.3 3.3 %collective-permute-done.26 = bf16[256,512]{1,0:T(8,128)(2,1)S(1)} collective-permute-done((bf16[256,512]{1,0:T(8,128)(2,1)S(1)}, bf16[256,512]{1,0:T(8,128)(2,1)S(1)}, u32[]{:S(2)}, u32[]{:S(2)}) %collective-permute-start.26) | collective-permute-done | bytes 262176 | tf_op jit(solution)/shard_map/ppermute | solution.py:17
  108.6 6.1 %collective-permute-done.27 = bf16[256,512]{1,0:T(8,128)(2,1)S(1)} collective-permute-done((bf16[256,512]{1,0:T(8,128)(2,1)S(1)}, bf16[256,512]{1,0:T(8,128)(2,1)S(1)}, u32[]{:S(2)}, u32[]{:S(2)}) %collective-permute-start.27) | collective-permute-done | bytes 262176 | tf_op jit(solution)/shard_map/ppermute | solution.py:17
  116.6 3.3 %collective-permute-done.33 = bf16[256,512]{1,0:T(8,128)(2,1)S(1)} collective-permute-done((bf16[256,512]{1,0:T(8,128)(2,1)S(1)}, bf16[256,512]{1,0:T(8,128)(2,1)S(1)}, u32[]{:S(2)}, u32[]{:S(2)}) %collective-permute-start.33) | collective-permute-done | bytes 262176 | tf_op jit(solution)/shard_map/ppermute | solution.py:17
  119.9 3.1 %collective-permute-done.34 = bf16[256,512]{1,0:T(8,128)(2,1)S(1)} collective-permute-done((bf16[256,512]{1,0:T(8,128)(2,1)S(1)}, bf16[256,512]{1,0:T(8,128)(2,1)S(1)}, u32[]{:S(2)}, u32[]{:S(2)}) %collective-permute-start.34) | collective-permute-done | bytes 262176 | tf_op jit(solution)/shard_map/ppermute | solution.py:17
  144.3 2.5 %collective-permute-start.31 = (bf16[64,512]{1,0:T(8,128)(2,1)S(1)}, bf16[64,512]{1,0:T(8,128)(2,1)S(1)}, u32[]{:S(2)}, u32[]{:S(2)}) collective-permute-start(bf16[64,512]{1,0:T(8,128)(2,1)S(1)} %get-tuple-element.63), channel_id=1, source_target_pairs={{0,4},{1,5},{2,6},{3,7},{4,0},{5,1},{6,2},{7,3},{8,12},{9,13},{10,... | collective-permute-start | bytes 196616 | tf_op jit(solution)/shard_map/ppermute | solution.py:17
  156.8 2.9 %collective-permute-done.39 = bf16[64,512]{1,0:T(8,128)(2,1)S(1)} collective-permute-done((bf16[64,512]{1,0:T(8,128)(2,1)S(1)}, bf16[64,512]{1,0:T(8,128)(2,1)S(1)}, u32[]{:S(2)}, u32[]{:S(2)}) %collective-permute-start.39) | collective-permute-done | bytes 65568 | tf_op jit(solution)/shard_map/ppermute | solution.py:17
  160.1 2.8 %collective-permute-start.24 = (bf16[64,1024]{1,0:T(8,128)(2,1)S(1)}, bf16[64,1024]{1,0:T(8,128)(2,1)S(1)}, u32[]{:S(2)}, u32[]{:S(2)}) collective-permute-start(bf16[64,1024]{1,0:T(8,128)(2,1)S(1)} %get-tuple-element.50), channel_id=1, source_target_pairs={{0,4},{1,5},{2,6},{3,7},{4,0},{5,1},{6,2},{7,3},{8,12},{9,13},{10,... | collective-permute-start | bytes 393224 | tf_op jit(solution)/shard_map/ppermute | solution.py:17
  164.7 2.8 %collective-permute-start.49 = (bf16[32,2048]{1,0:T(8,128)(2,1)S(1)}, bf16[32,2048]{1,0:T(8,128)(2,1)S(1)}, u32[]{:S(2)}, u32[]{:S(2)}) collective-permute-start(bf16[32,2048]{1,0:T(8,128)(2,1)S(1)} %get-tuple-element.57), channel_id=1, source_target_pairs={{0,4},{1,5},{2,6},{3,7},{4,0},{5,1},{6,2},{7,3},{8,12},{9,13},{10,... | collective-permute-start | bytes 393224 | tf_op jit(solution)/shard_map/ppermute | solution.py:17
  173.1 9.7 %collective-permute-start.56 = (bf16[32,2048]{1,0:T(8,128)(2,1)S(1)}, bf16[32,2048]{1,0:T(8,128)(2,1)S(1)}, u32[]{:S(2)}, u32[]{:S(2)}) collective-permute-start(bf16[32,2048]{1,0:T(8,128)(2,1)S(1)} %get-tuple-element.60), channel_id=1, source_target_pairs={{0,4},{1,5},{2,6},{3,7},{4,0},{5,1},{6,2},{7,3},{8,12},{9,13},{10,... | collective-permute-start | bytes 393224 | tf_op jit(solution)/shard_map/ppermute | solution.py:17
  184.7 7.7 %collective-permute-done.56 = bf16[32,2048]{1,0:T(8,128)(2,1)S(1)} collective-permute-done((bf16[32,2048]{1,0:T(8,128)(2,1)S(1)}, bf16[32,2048]{1,0:T(8,128)(2,1)S(1)}, u32[]{:S(2)}, u32[]{:S(2)}) %collective-permute-start.56) | collective-permute-done | bytes 131104 | tf_op jit(solution)/shard_map/ppermute | solution.py:17
  (187 shorter events, 78.6 us)
Async XLA Ops:
  2.6 24.3 %collective-permute-start.3 = (bf16[64,2048]{1,0:T(8,128)(2,1)S(1)}, bf16[64,2048]{1,0:T(8,128)(2,1)S(1)}, u32[]{:S(2)}, u32[]{:S(2)}) collective-permute-start(bf16[64,2048]{1,0:T(8,128)(2,1)S(1)} %get-tuple-element.52), channel_id=1, source_target_pairs={{0,2},{1,3},{2,0},{3,1},{4,6},{5,7},{6,4},{7,5},{8,10},{9,11},{10,... | collective-permute-start | bytes 786440 | tf_op jit(solution)/shard_map/ppermute | solution.py:17
  5.7 21.8 %collective-permute-start.4 = (bf16[64,2048]{1,0:T(8,128)(2,1)S(1)}, bf16[64,2048]{1,0:T(8,128)(2,1)}, u32[]{:S(2)}, u32[]{:S(2)}) collective-permute-start(bf16[64,2048]{1,0:T(8,128)(2,1)S(1)} %get-tuple-element.52), channel_id=1, source_target_pairs={{0,4},{1,5},{2,6},{3,7},{4,0},{5,1},{6,2},{7,3},{8,12},{9,13},{10,... | collective-permute-start | bytes 786440 | tf_op jit(solution)/shard_map/ppermute | solution.py:17
  8.2 20.7 %collective-permute-start.5 = (bf16[64,2048]{1,0:T(8,128)(2,1)S(1)}, bf16[64,2048]{1,0:T(8,128)(2,1)S(1)}, u32[]{:S(2)}, u32[]{:S(2)}) collective-permute-start(bf16[64,2048]{1,0:T(8,128)(2,1)S(1)} %get-tuple-element.52), channel_id=1, source_target_pairs={{0,6},{1,7},{2,4},{3,5},{4,2},{5,3},{6,0},{7,1},{8,14},{9,15},{10,... | collective-permute-start | bytes 786440 | tf_op jit(solution)/shard_map/ppermute | solution.py:17
  10.7 22.0 %collective-permute-start.40 = (bf16[64,2048]{1,0:T(8,128)(2,1)}, bf16[64,2048]{1,0:T(8,128)(2,1)}, u32[]{:S(2)}, u32[]{:S(2)}) collective-permute-start(bf16[64,2048]{1,0:T(8,128)(2,1)} %get-tuple-element.53), channel_id=1, source_target_pairs={{0,2},{1,3},{2,0},{3,1},{4,6},{5,7},{6,4},{7,5},{8,10},{9,11},{10,... | collective-permute-start | bytes 786440 | tf_op jit(solution)/shard_map/ppermute | solution.py:17
  23.4 19.2 %collective-permute-start.41 = (bf16[64,2048]{1,0:T(8,128)(2,1)}, bf16[64,2048]{1,0:T(8,128)(2,1)}, u32[]{:S(2)}, u32[]{:S(2)}) collective-permute-start(bf16[64,2048]{1,0:T(8,128)(2,1)} %get-tuple-element.53), channel_id=1, source_target_pairs={{0,4},{1,5},{2,6},{3,7},{4,0},{5,1},{6,2},{7,3},{8,12},{9,13},{10,... | collective-permute-start | bytes 786440 | tf_op jit(solution)/shard_map/ppermute | solution.py:17
  26.9 27.4 %collective-permute-start.7 = (bf16[256,2048]{1,0:T(8,128)(2,1)}, bf16[256,2048]{1,0:T(8,128)(2,1)}, u32[]{:S(2)}, u32[]{:S(2)}) collective-permute-start(bf16[256,2048]{1,0:T(8,128)(2,1)} %get-tuple-element.33), channel_id=1, source_target_pairs={{0,8},{8,0},{16,24},{24,16},{1,9},{9,1},{17,25},{25,17},{2,10},{10... | collective-permute-start | bytes 3145736 | tf_op jit(solution)/shard_map/ppermute | solution.py:17
  27.4 38.3 %collective-permute-start.8 = (bf16[256,2048]{1,0:T(8,128)(2,1)}, bf16[256,2048]{1,0:T(8,128)(2,1)}, u32[]{:S(2)}, u32[]{:S(2)}) collective-permute-start(bf16[256,2048]{1,0:T(8,128)(2,1)} %get-tuple-element.35), channel_id=1, source_target_pairs={{0,16},{8,24},{16,0},{24,8},{1,17},{9,25},{17,1},{25,9},{2,18},{10... | collective-permute-start | bytes 3145736 | tf_op jit(solution)/shard_map/ppermute | solution.py:17
  29.0 47.8 %collective-permute-start.9 = (bf16[256,2048]{1,0:T(8,128)(2,1)S(1)}, bf16[256,2048]{1,0:T(8,128)(2,1)}, u32[]{:S(2)}, u32[]{:S(2)}) collective-permute-start(bf16[256,2048]{1,0:T(8,128)(2,1)S(1)} %get-tuple-element.34), channel_id=1, source_target_pairs={{0,24},{8,16},{16,8},{24,0},{1,25},{9,17},{17,9},{25,1},{2,26},{10... | collective-permute-start | bytes 3145736 | tf_op jit(solution)/shard_map/ppermute | solution.py:17
  32.7 46.3 %collective-permute-start.6 = (bf16[4,64,2048]{2,1,0:T(8,128)(2,1)}, bf16[4,64,2048]{2,1,0:T(8,128)(2,1)}, u32[]{:S(2)}, u32[]{:S(2)}) collective-permute-start(bf16[4,64,2048]{2,1,0:T(8,128)(2,1)} %get-tuple-element.37), channel_id=1, source_target_pairs={{0,1},{1,0},{2,3},{3,2},{4,5},{5,4},{6,7},{7,6},{8,9},{9,8},{10,11... | collective-permute-start | bytes 3145736 | tf_op jit(solution)/shard_map/ppermute | solution.py:17
  51.7 49.2 %collective-permute-start.16 = (bf16[256,512]{1,0:T(8,128)(2,1)}, bf16[256,512]{1,0:T(8,128)(2,1)S(1)}, u32[]{:S(2)}, u32[]{:S(2)}) collective-permute-start(bf16[256,512]{1,0:T(8,128)(2,1)} %get-tuple-element.28), channel_id=1, source_target_pairs={{0,8},{8,0},{16,24},{24,16},{1,9},{9,1},{17,25},{25,17},{2,10},{10... | collective-permute-start | bytes 786440 | tf_op jit(solution)/shard_map/ppermute | solution.py:17
  54.4 49.5 %collective-permute-start.17 = (bf16[256,512]{1,0:T(8,128)(2,1)S(1)}, bf16[256,512]{1,0:T(8,128)(2,1)S(1)}, u32[]{:S(2)}, u32[]{:S(2)}) collective-permute-start(bf16[256,512]{1,0:T(8,128)(2,1)S(1)} %copy-done.15), channel_id=1, source_target_pairs={{0,16},{8,24},{16,0},{24,8},{1,17},{9,25},{17,1},{25,9},{2,18},{10... | collective-permute-start | bytes 786440 | tf_op jit(solution)/shard_map/ppermute | solution.py:17
  65.8 19.9 %collective-permute-start.19 = (bf16[256,512]{1,0:T(8,128)(2,1)S(1)}, bf16[256,512]{1,0:T(8,128)(2,1)S(1)}, u32[]{:S(2)}, u32[]{:S(2)}) collective-permute-start(bf16[256,512]{1,0:T(8,128)(2,1)S(1)} %copy-done.18), channel_id=1, source_target_pairs={{0,8},{8,0},{16,24},{24,16},{1,9},{9,1},{17,25},{25,17},{2,10},{10... | collective-permute-start | bytes 786440 | tf_op jit(solution)/shard_map/ppermute | solution.py:17
  79.1 20.4 %collective-permute-start.20 = (bf16[256,512]{1,0:T(8,128)(2,1)S(1)}, bf16[256,512]{1,0:T(8,128)(2,1)S(1)}, u32[]{:S(2)}, u32[]{:S(2)}) collective-permute-start(bf16[256,512]{1,0:T(8,128)(2,1)S(1)} %copy-done.17), channel_id=1, source_target_pairs={{0,16},{8,24},{16,0},{24,8},{1,17},{9,25},{17,1},{25,9},{2,18},{10... | collective-permute-start | bytes 786440 | tf_op jit(solution)/shard_map/ppermute | solution.py:17
  83.6 16.4 %collective-permute-start.21 = (bf16[256,512]{1,0:T(8,128)(2,1)S(1)}, bf16[256,512]{1,0:T(8,128)(2,1)S(1)}, u32[]{:S(2)}, u32[]{:S(2)}) collective-permute-start(bf16[256,512]{1,0:T(8,128)(2,1)S(1)} %copy-done.16), channel_id=1, source_target_pairs={{0,24},{8,16},{16,8},{24,0},{1,25},{9,17},{17,9},{25,1},{2,26},{10... | collective-permute-start | bytes 786440 | tf_op jit(solution)/shard_map/ppermute | solution.py:17
  86.3 18.1 %collective-permute-start.18 = (bf16[256,512]{1,0:T(8,128)(2,1)S(1)}, bf16[256,512]{1,0:T(8,128)(2,1)S(1)}, u32[]{:S(2)}, u32[]{:S(2)}) collective-permute-start(bf16[256,512]{1,0:T(8,128)(2,1)S(1)} %copy-done.14), channel_id=1, source_target_pairs={{0,24},{8,16},{16,8},{24,0},{1,25},{9,17},{17,9},{25,1},{2,26},{10... | collective-permute-start | bytes 786440 | tf_op jit(solution)/shard_map/ppermute | solution.py:17
  100.0 14.8 %collective-permute-start.27 = (bf16[256,512]{1,0:T(8,128)(2,1)S(1)}, bf16[256,512]{1,0:T(8,128)(2,1)S(1)}, u32[]{:S(2)}, u32[]{:S(2)}) collective-permute-start(bf16[256,512]{1,0:T(8,128)(2,1)S(1)} %copy-done.12), channel_id=1, source_target_pairs={{0,16},{8,24},{16,0},{24,8},{1,17},{9,25},{17,1},{25,9},{2,18},{10... | collective-permute-start | bytes 786440 | tf_op jit(solution)/shard_map/ppermute | solution.py:17
  103.9 16.0 %collective-permute-start.33 = (bf16[256,512]{1,0:T(8,128)(2,1)S(1)}, bf16[256,512]{1,0:T(8,128)(2,1)S(1)}, u32[]{:S(2)}, u32[]{:S(2)}) collective-permute-start(bf16[256,512]{1,0:T(8,128)(2,1)S(1)} %copy-done.10), channel_id=1, source_target_pairs={{0,8},{8,0},{16,24},{24,16},{1,9},{9,1},{17,25},{25,17},{2,10},{10... | collective-permute-start | bytes 786440 | tf_op jit(solution)/shard_map/ppermute | solution.py:17
  104.5 18.5 %collective-permute-start.34 = (bf16[256,512]{1,0:T(8,128)(2,1)S(1)}, bf16[256,512]{1,0:T(8,128)(2,1)S(1)}, u32[]{:S(2)}, u32[]{:S(2)}) collective-permute-start(bf16[256,512]{1,0:T(8,128)(2,1)S(1)} %copy-done.8), channel_id=1, source_target_pairs={{0,16},{8,24},{16,0},{24,8},{1,17},{9,25},{17,1},{25,9},{2,18},{10... | collective-permute-start | bytes 786440 | tf_op jit(solution)/shard_map/ppermute | solution.py:17
  139.1 20.6 %collective-permute-start.22 = (bf16[4,64,1024]{2,1,0:T(8,128)(2,1)S(1)}, bf16[4,64,1024]{2,1,0:T(8,128)(2,1)S(1)}, u32[]{:S(2)}, u32[]{:S(2)}) collective-permute-start(bf16[4,64,1024]{2,1,0:T(8,128)(2,1)S(1)} %fusion.42), channel_id=1, source_target_pairs={{0,1},{1,0},{2,3},{3,2},{4,5},{5,4},{6,7},{7,6},{8,9},{9,8},{10,11... | collective-permute-start | bytes 1572872 | tf_op jit(solution)/shard_map/ppermute | solution.py:17
  141.1 23.3 %collective-permute-start.47 = (bf16[4,32,2048]{2,1,0:T(8,128)(2,1)S(1)}, bf16[4,32,2048]{2,1,0:T(8,128)(2,1)S(1)}, u32[]{:S(2)}, u32[]{:S(2)}) collective-permute-start(bf16[4,32,2048]{2,1,0:T(8,128)(2,1)S(1)} %fusion.43), channel_id=1, source_target_pairs={{0,1},{1,0},{2,3},{3,2},{4,5},{5,4},{6,7},{7,6},{8,9},{9,8},{10,11... | collective-permute-start | bytes 1572872 | tf_op jit(solution)/shard_map/ppermute | solution.py:17
  164.6 18.3 %collective-permute-start.48 = (bf16[32,2048]{1,0:T(8,128)(2,1)S(1)}, bf16[32,2048]{1,0:T(8,128)(2,1)S(1)}, u32[]{:S(2)}, u32[]{:S(2)}) collective-permute-start(bf16[32,2048]{1,0:T(8,128)(2,1)S(1)} %get-tuple-element.55), channel_id=1, source_target_pairs={{0,2},{1,3},{2,0},{3,1},{4,6},{5,7},{6,4},{7,5},{8,10},{9,11},{10,... | collective-permute-start | bytes 393224 | tf_op jit(solution)/shard_map/ppermute | solution.py:17
  164.7 19.9 %collective-permute-start.49 = (bf16[32,2048]{1,0:T(8,128)(2,1)S(1)}, bf16[32,2048]{1,0:T(8,128)(2,1)S(1)}, u32[]{:S(2)}, u32[]{:S(2)}) collective-permute-start(bf16[32,2048]{1,0:T(8,128)(2,1)S(1)} %get-tuple-element.57), channel_id=1, source_target_pairs={{0,4},{1,5},{2,6},{3,7},{4,0},{5,1},{6,2},{7,3},{8,12},{9,13},{10,... | collective-permute-start | bytes 393224 | tf_op jit(solution)/shard_map/ppermute | solution.py:17
  168.4 16.3 %collective-permute-start.50 = (bf16[32,2048]{1,0:T(8,128)(2,1)S(1)}, bf16[32,2048]{1,0:T(8,128)(2,1)S(1)}, u32[]{:S(2)}, u32[]{:S(2)}) collective-permute-start(bf16[32,2048]{1,0:T(8,128)(2,1)S(1)} %get-tuple-element.56), channel_id=1, source_target_pairs={{0,6},{1,7},{2,4},{3,5},{4,2},{5,3},{6,0},{7,1},{8,14},{9,15},{10,... | collective-permute-start | bytes 393224 | tf_op jit(solution)/shard_map/ppermute | solution.py:17
  173.1 19.3 %collective-permute-start.56 = (bf16[32,2048]{1,0:T(8,128)(2,1)S(1)}, bf16[32,2048]{1,0:T(8,128)(2,1)S(1)}, u32[]{:S(2)}, u32[]{:S(2)}) collective-permute-start(bf16[32,2048]{1,0:T(8,128)(2,1)S(1)} %get-tuple-element.60), channel_id=1, source_target_pairs={{0,4},{1,5},{2,6},{3,7},{4,0},{5,1},{6,2},{7,3},{8,12},{9,13},{10,... | collective-permute-start | bytes 393224 | tf_op jit(solution)/shard_map/ppermute | solution.py:17
  (53 other events, 423.5 us)
